TPU v7x, 32 devices: a whole 2x2x4 slice. The times are simulated.
32 devices in a mesh: groups: 2 (over y), snap: 4 (over z), slab: 2 (over x), sub: 2 (over core).
Axes of the slice: x: 2, y: 2, z: 4, core: 2. Of those that a mesh axis runs over, the one named last changes fastest.
Arguments:
- fields: float32 [8, 4, 4, 16, 128], P(('groups', 'snap'), None, 'slab', 'sub'), parts along dimension 0, may hold values from -18 to 18
- snap_ids: int32 [8], P(('groups', 'snap')), parts along dimension 0, may hold values from 0 to 63
- snap_weight: float32 [64], replicated, may hold values from 0.5 to 2
- product_terms: int32 [192, 3], replicated, may hold values from 0 to 27, as said below
- mix_weight: float32 [192], replicated, may hold values from -1.5 to 1.5
Outputs:
- whitened: bfloat16 [8, 192, 4, 16, 128], P(('groups', 'snap'), None, 'slab', 'sub'), parts along dimension 0
- r_factor: float32 [384, 192], P('groups'), parts along dimension 0
There are 2 independent parts, one for each index of `groups`. A program takes and returns all parts, laid end to end along the dimension named above; an argument that names none is the same for every part. Nothing has to cross between parts.
Inputs may be any that keep to these rules, and one draw needn't show every extreme that they name: `product_terms`: each row names three different bases, and no two rows are equal.
All inputs are finite; a program needn't handle non-finite values.
Results may differ from a plain program's by a relative error of at most 0.0028.
Values sent between devices are 32-bit elements; how exact they have to be, the bound alone decides.
A program may use at most 64 MiB of HBM per device.

v0:
```python
import jax
import jax.numpy as jnp
from jax import lax
from jax.sharding import PartitionSpec as P

ridge_value = 0.05


def padded_2(block, sides, width):
    for axis, dim in sides:
        count = lax.axis_size(axis)
        forward = [(i, i + 1) for i in range(count - 1)]
        forward.append((count - 1, 0))
        backward = [(target, source) for source, target in forward]
        low = lax.ppermute(
            lax.slice_in_dim(block, block.shape[dim] - width, None, axis=dim), axis, forward
        )
        high = lax.ppermute(lax.slice_in_dim(block, 0, width, axis=dim), axis, backward)
        block = jnp.concatenate([low, block, high], axis=dim)
    return block


def stencil_pair(values, ahead_one, behind_one, ahead_two, behind_two):
    first_deriv = (8.0 * (ahead_one - behind_one) - (ahead_two - behind_two)) / 12.0
    second_deriv = (
        16.0 * (ahead_one + behind_one) - (ahead_two + behind_two) - 30.0 * values
    ) / 12.0
    return (first_deriv, second_deriv)


def dot_highest(left_matrix, right_matrix):
    return jnp.dot(left_matrix, right_matrix, precision=lax.Precision.HIGHEST)


def upper_cholesky(matrix):
    order = matrix.shape[0]
    positions = jnp.arange(order, dtype=jnp.int32)

    def column_step(step, state):
        work, upper = state
        row_now = lax.dynamic_slice_in_dim(work, step, 1, 0)[0]
        pivot = lax.dynamic_slice_in_dim(row_now, step, 1, 0)[0]
        scaled = jnp.where(positions >= step, row_now / jnp.sqrt(pivot), 0.0)
        work = work - scaled[:, None] * scaled[None, :]
        upper = lax.dynamic_update_slice_in_dim(upper, scaled[None, :], step, 0)
        return (work, upper)

    start = (matrix, jnp.zeros_like(matrix))
    return lax.fori_loop(0, order, column_step, start)[1]


def transposed_solve(upper, right_side):
    order = upper.shape[0]
    positions = jnp.arange(order, dtype=jnp.int32)

    def row_step(step, solved):
        column = lax.dynamic_slice_in_dim(upper, step, 1, 1)[:, 0]
        pivot = lax.dynamic_slice_in_dim(column, step, 1, 0)[0]
        masked = jnp.where(positions < step, column, 0.0)
        target = lax.dynamic_slice_in_dim(right_side, step, 1, 0)
        row_new = (target - dot_highest(masked[None, :], solved)) / pivot
        return lax.dynamic_update_slice_in_dim(solved, row_new, step, 0)

    return lax.fori_loop(0, order, row_step, jnp.zeros_like(right_side))


def local(fields, snap_ids, snap_weight, product_terms, mix_weight):
    padded = padded_2(fields, (("slab", 2), ("sub", 3)), 2)
    layers = fields.shape[2]
    columns = fields.shape[3]
    center = padded[0, :, 2 : 2 + layers, 2 : 2 + columns, :]

    def along_z(offset):
        return padded[0, :, 2 + offset : 2 + offset + layers, 2 : 2 + columns, :]

    def along_x(offset):
        return padded[0, :, 2 : 2 + layers, 2 + offset : 2 + offset + columns, :]

    z_first, z_second = stencil_pair(center, along_z(1), along_z(-1), along_z(2), along_z(-2))
    x_first, x_second = stencil_pair(center, along_x(1), along_x(-1), along_x(2), along_x(-2))
    y_first, y_second = stencil_pair(
        center,
        jnp.roll(center, -1, 3),
        jnp.roll(center, 1, 3),
        jnp.roll(center, -2, 3),
        jnp.roll(center, 2, 3),
    )
    stacked = jnp.stack([center, z_first, x_first, y_first, z_second, x_second, y_second], axis=1)
    base_count = stacked.shape[0] * stacked.shape[1]
    bases = stacked.reshape(base_count, -1)
    table_size = snap_weight.shape[0]
    snap_scale = jnp.sum(jnp.where(jnp.arange(table_size) == snap_ids[0], snap_weight, 0.0))
    feature_count = product_terms.shape[0]
    choose = (product_terms.T.reshape(-1)[:, None] == jnp.arange(base_count)[None, :]).astype(
        jnp.float32
    )
    picked = dot_highest(choose, bases)
    left_term = picked[:feature_count]
    middle = picked[feature_count : 2 * feature_count]
    right_term = picked[2 * feature_count :]
    features = snap_scale * left_term * (middle + mix_weight[:, None] * right_term)
    local_gram = lax.dot_general(
        features, features, (((1,), (1,)), ((), ())), precision=lax.Precision.HIGHEST
    )
    cells_total = float(
        lax.axis_size("snap") * lax.axis_size("slab") * lax.axis_size("sub") * bases.shape[1]
    )
    identity = jnp.eye(feature_count, dtype=jnp.float32)
    total_gram = lax.psum(local_gram, ("snap", "slab", "sub"))
    r_factor = upper_cholesky(total_gram / cells_total + ridge_value * identity)
    inverse = transposed_solve(r_factor, identity)
    solved = dot_highest(inverse, features)
    whitened = solved.reshape(1, feature_count, layers, columns, -1).astype(jnp.bfloat16)
    return (whitened, r_factor)


def solution(mesh):
    return jax.shard_map(
        local,
        mesh=mesh,
        in_specs=(
            P(("groups", "snap"), None, "slab", "sub", None),
            P(("groups", "snap")),
            P(),
            P(),
            P(),
        ),
        out_specs=(P(("groups", "snap"), None, "slab", "sub", None), P("groups", None)),
        check_vma=False,
    )
```

profile of v0, /device:TPU:0, one launch (start us, length us, event | category | flops | bytes accessed | tf_op | source)
XLA Modules:
  0.0 691.6 jit_solution(17361808163700659640)
XLA Ops:
  7.2 3.0 collective-permute-start.1
  10.3 0.8 bitcast_dynamic-update-slice_fusion.2
  11.1 0.9 slice_bitcast_fusion.7
  12.0 0.9 slice_bitcast_fusion.6
  12.9 0.9 slice_bitcast_fusion.3
  13.9 0.9 slice_bitcast_fusion.2
  15.4 1.3 fusion.15
  16.7 0.8 eq.29
  17.5 0.8 constant_dynamic-update-slice_fusion.1
  18.8 0.7 bitcast_dynamic-update-slice_fusion.1
  20.1 2.1 fusion.8
  22.2 1.0 fusion.6
  23.2 2.1 fusion.17
  25.3 92.5 %all-reduce.2.cloned.1.call-done = f32[192,192]{1,0:T(8,128)} async-done(((f32[192,192]{1,0:T(8,128)}), f32[192,192]{1,0:T(8,128)}) %all-reduce.2.cloned.1.call-update) | async-done | bytes 147472 | tf_op jit(solution)/shard_map/psum | solution.py:109
  117.8 0.9 select_add_fusion
  118.8 288.9 %while.36 = (s32[]{:T(128)}, f32[192,192]{1,0:T(8,128)S(1)}, f32[192,192]{1,0:T(8,128)S(1)}, s32[]{:T(128)}, s32[]{:T(128)}, /*index=5*/s32[]{:T(128)}) while((s32[]{:T(128)}, f32[192,192]{1,0:T(8,128)S(1)}, f32[192,192]{1,0:T(8,128)S(1)}, s32[]{:T(128)}, s32[]{:T(128)}, /*index=5*/s32[]{:T(128)}) %tuple.96), condition=%wide.region_3.4_spmd.clone, body=%wide.region_2.3_spmd.clone.sunk | while | flops 74691 | bytes 302333 | solution.py:49
  407.9 274.4 %while.37 = (s32[]{:T(128)}, f32[192,192]{1,0:T(8,128)S(1)}, f32[192,192]{1,0:T(8,128)S(1)}, f32[192,192]{0,1:T(8,128)S(1)}, s32[]{:T(128)}, /*index=5*/s32[]{:T(128)}, s32[]{:T(128)}) while((s32[]{:T(128)}, f32[192,192]{1,0:T(8,128)S(1)}, f32[192,192]{1,0:T(8,128)S(1)}, f32[192,192]{0,1:T(8,128)S(1)}, s32[]{:T(128)}, ...), condition=%wide.region_5.6_spmd.clone, body=%wide.region_4.5_spmd.clone.sunk | while | flops 443139 | bytes 154493 | solution.py:64
  411.4 0.7 fusion.30
  415.7 0.7 fusion.30
  418.5 0.7 fusion.30
  422.8 0.7 fusion.30
  427.1 0.7 fusion.30
  682.2 1.5 fusion.7
  683.7 1.1 copy.23
  (2136 shorter events, 409.5 us)
Async XLA Ops:
  7.2 12.7 %copy-start = (f32[1,4,2,8,128]{4,3,2,1,0:T(8,128)S(1)}, f32[1,4,2,8,128]{4,3,2,1,0:T(8,128)}, u32[]{:S(2)}) copy-start(f32[1,4,2,8,128]{4,3,2,1,0:T(8,128)} %param.9) | copy-start | bytes 98308
  7.2 110.7 %all-reduce.2.cloned.1.call-start = ((), (), s32[]{:S(2)}) async-start(), calls=%async_computation | async-start | bytes 393216 | tf_op jit(solution)/shard_map/psum | solution.py:109
  7.2 10.2 %collective-permute-start.1 = (f32[1,4,2,8,128]{4,3,2,1,0:T(8,128)}, f32[1,4,2,8,128]{4,3,2,1,0:T(8,128)S(1)}, u32[]{:S(2)}, u32[]{:S(2)}) collective-permute-start(f32[1,4,2,8,128]{4,3,2,1,0:T(8,128)} %param.9), channel_id=1, source_target_pairs={{0,2},{2,0},{1,3},{3,1},{4,6},{6,4},{5,7},{7,5},{8,10},{10,8},{9,1... | collective-permute-start | bytes 98312 | tf_op jit(solution)/shard_map/ppermute | solution.py:15
  10.3 8.0 %collective-permute-start = (f32[1,4,2,8,128]{4,3,2,1,0:T(8,128)}, f32[1,4,2,8,128]{4,3,2,1,0:T(8,128)S(1)}, u32[]{:S(2)}, u32[]{:S(2)}) collective-permute-start(f32[1,4,2,8,128]{4,3,2,1,0:T(8,128)} %param.9), channel_id=1, source_target_pairs={{2,0},{0,2},{3,1},{1,3},{6,4},{4,6},{7,5},{5,7},{10,8},{8,10},{11,... | collective-permute-start | bytes 98312 | tf_op jit(solution)/shard_map/ppermute | solution.py:18
  18.3 1.3 collective-permute-start.2
  18.3 1.3 collective-permute-start.3
  20.1 2.1 copy-start.2
  407.7 276.0 %copy-start.1 = (f32[192,192]{1,0:T(8,128)}, f32[192,192]{1,0:T(8,128)S(1)}, u32[]{:S(2)}) copy-start(f32[192,192]{1,0:T(8,128)S(1)} %get-tuple-element.297) | copy-start | bytes 442372
Sparse Core Ops, SparseCore 0:
  25.4 92.3 all-reduce.1
where the time goes:
time: 696 us; the launch traced here: 692 us
  local copies, waits for them, and re-layouts  254 us (36%)
  loops' own time  151 us (22%)
  matrix products  146 us (21%)
  waiting for transfers between devices  92.6 us (13%)
  other arithmetic  29.2 us (4%)
  between operations  14.9 us (2%)
    dot_general x194, matrix products, dot_highest(): return jnp.dot(left_matrix, right_matrix, precision=lax.Precision.HIGHEST)  144 us
    another operation x1, loops' own time, upper_cholesky(): return lax.fori_loop(0, order, column_step, start)[1]  143 us
    dynamic_slice x192, local copies, waits for them, and re-layouts, row_step(): pivot = lax.dynamic_slice_in_dim(column, step, 1, 0)[0]  114 us
    dynamic_slice x192, local copies, waits for them, and re-layouts, column_step(): pivot = lax.dynamic_slice_in_dim(row_now, step, 1, 0)[0]  113 us
    psum x1, waiting for transfers between devices, local(): total_gram = lax.psum(local_gram, ('snap', 'slab', 'sub'))  92.5 us
    sub x192, other arithmetic, column_step(): work = work - scaled[:, None] * scaled[None, :]  19.5 us
  transfers between devices with their start and end apart: 5, of which 2 were waited for; matrix products, arithmetic and copies ran while one was open for 1% of the time, Pallas kernels for 0%

commit v1 on v0

--- a/solution.py
+++ b/solution.py
@@ -106,7 +106,7 @@
         lax.axis_size("snap") * lax.axis_size("slab") * lax.axis_size("sub") * bases.shape[1]
     )
     identity = jnp.eye(feature_count, dtype=jnp.float32)
-    total_gram = lax.psum(local_gram, ("snap", "slab", "sub"))
+    total_gram = lax.psum(lax.psum(local_gram, ("slab", "sub")), "snap")
     r_factor = upper_cholesky(total_gram / cells_total + ridge_value * identity)
     inverse = transposed_solve(r_factor, identity)
     solved = dot_highest(inverse, features)

time: 696 us -> 658 us (0.945)
  waiting for transfers between devices: 92.6 us -> 71.2 us
  loops' own time: 151 us -> 135 us
    psum x1 -> x2, waiting for transfers between devices: 92.5 us -> 71.1 us  [local(): total_gram = lax.psum(lax.psum(local_gram, ('slab', 'sub')), 'snap')]
    another operation x1, loops' own time: 143 us -> 127 us  [upper_cholesky(): return lax.fori_loop(0, order, column_step, start)[1]]
  transfers between devices with their start and end apart: 5 -> 6, of which waited for: 2 -> 3; matrix products, arithmetic and copies ran while one was open for 1% -> 1% of each run, Pallas kernels for 0% -> 0%
where the time goes in v1:
time: 658 us; the launch traced here: 655 us
  local copies, waits for them, and re-layouts  254 us (39%)
  matrix products  146 us (22%)
  loops' own time  135 us (21%)
  waiting for transfers between devices  71.2 us (11%)
  other arithmetic  29.3 us (4%)
  between operations  14.9 us (2%)
    dot_general x194, matrix products, dot_highest(): return jnp.dot(left_matrix, right_matrix, precision=lax.Precision.HIGHEST)  144 us
    another operation x1, loops' own time, upper_cholesky(): return lax.fori_loop(0, order, column_step, start)[1]  127 us
    dynamic_slice x192, local copies, waits for them, and re-layouts, column_step(): pivot = lax.dynamic_slice_in_dim(row_now, step, 1, 0)[0]  114 us
    dynamic_slice x192, local copies, waits for them, and re-layouts, row_step(): pivot = lax.dynamic_slice_in_dim(column, step, 1, 0)[0]  114 us
    psum x2, waiting for transfers between devices, local(): total_gram = lax.psum(lax.psum(local_gram, ('slab', 'sub')), 'snap')  71.1 us
    sub x192, other arithmetic, column_step(): work = work - scaled[:, None] * scaled[None, :]  19.5 us
  transfers between devices with their start and end apart: 6, of which 3 were waited for; matrix products, arithmetic and copies ran while one was open for 1% of the time, Pallas kernels for 0%

profile of v1, /device:TPU:0, one launch (start us, length us, event | category | flops | bytes accessed | tf_op | source)
XLA Modules:
  0.0 654.6 jit_solution(13722193272102669698)
XLA Ops:
  7.2 3.0 collective-permute-start.1
  10.3 0.8 bitcast_dynamic-update-slice_fusion.2
  11.1 0.9 slice_bitcast_fusion.7
  12.0 0.9 slice_bitcast_fusion.6
  12.9 0.9 slice_bitcast_fusion.3
  13.9 0.9 slice_bitcast_fusion.2
  15.4 1.3 fusion.15
  16.7 0.8 eq.29
  17.5 0.8 constant_dynamic-update-slice_fusion.1
  18.8 0.7 bitcast_dynamic-update-slice_fusion.1
  20.1 2.1 fusion.8
  22.2 1.1 fusion.6
  23.3 2.1 fusion.17
  25.5 33.8 %all-reduce.3.cloned.1.call-done = f32[192,192]{1,0:T(8,128)} async-done(((f32[192,192]{1,0:T(8,128)}), f32[192,192]{1,0:T(8,128)}) %all-reduce.3.cloned.1.call-update) | async-done | bytes 147472 | tf_op jit(solution)/shard_map/psum | solution.py:109
  59.3 37.3 %all-reduce.5.cloned.1.call-done = f32[192,192]{1,0:T(8,128)} async-done(((f32[192,192]{1,0:T(8,128)}), f32[192,192]{1,0:T(8,128)}) %all-reduce.5.cloned.1.call-update) | async-done | bytes 147472 | tf_op jit(solution)/shard_map/psum | solution.py:109
  96.6 0.9 select_add_fusion
  97.6 273.1 %while.36 = (s32[]{:T(128)}, f32[192,192]{1,0:T(8,128)S(1)}, f32[192,192]{1,0:T(8,128)S(1)}, s32[]{:T(128)}, s32[]{:T(128)}, /*index=5*/s32[]{:T(128)}) while((s32[]{:T(128)}, f32[192,192]{1,0:T(8,128)S(1)}, f32[192,192]{1,0:T(8,128)S(1)}, s32[]{:T(128)}, s32[]{:T(128)}, /*index=5*/s32[]{:T(128)}) %tuple.96), condition=%wide.region_4.5_spmd.clone, body=%wide.region_3.4_spmd.clone.sunk | while | flops 74691 | bytes 302333 | solution.py:49
  370.9 274.4 %while.37 = (s32[]{:T(128)}, f32[192,192]{1,0:T(8,128)S(1)}, f32[192,192]{1,0:T(8,128)S(1)}, f32[192,192]{0,1:T(8,128)S(1)}, s32[]{:T(128)}, /*index=5*/s32[]{:T(128)}, s32[]{:T(128)}) while((s32[]{:T(128)}, f32[192,192]{1,0:T(8,128)S(1)}, f32[192,192]{1,0:T(8,128)S(1)}, f32[192,192]{0,1:T(8,128)S(1)}, s32[]{:T(128)}, ...), condition=%wide.region_6.7_spmd.clone, body=%wide.region_5.6_spmd.clone.sunk | while | flops 443139 | bytes 154493 | solution.py:64
  371.5 0.7 fusion.30
  375.8 0.7 fusion.30
  380.1 0.7 fusion.30
  383.0 0.7 fusion.30
  645.3 1.5 fusion.7
  646.7 1.1 copy.23
  (2139 shorter events, 410.8 us)
Async XLA Ops:
  7.2 12.7 %copy-start = (f32[1,4,2,8,128]{4,3,2,1,0:T(8,128)S(1)}, f32[1,4,2,8,128]{4,3,2,1,0:T(8,128)}, u32[]{:S(2)}) copy-start(f32[1,4,2,8,128]{4,3,2,1,0:T(8,128)} %param.9) | copy-start | bytes 98308
  7.2 52.1 %all-reduce.3.cloned.1.call-start = ((), (), s32[]{:S(2)}) async-start(), calls=%async_computation | async-start | bytes 393216 | tf_op jit(solution)/shard_map/psum | solution.py:109
  7.2 10.2 %collective-permute-start.1 = (f32[1,4,2,8,128]{4,3,2,1,0:T(8,128)}, f32[1,4,2,8,128]{4,3,2,1,0:T(8,128)S(1)}, u32[]{:S(2)}, u32[]{:S(2)}) collective-permute-start(f32[1,4,2,8,128]{4,3,2,1,0:T(8,128)} %param.9), channel_id=1, source_target_pairs={{0,2},{2,0},{1,3},{3,1},{4,6},{6,4},{5,7},{7,5},{8,10},{10,8},{9,1... | collective-permute-start | bytes 98312 | tf_op jit(solution)/shard_map/ppermute | solution.py:15
  10.3 8.0 %collective-permute-start = (f32[1,4,2,8,128]{4,3,2,1,0:T(8,128)}, f32[1,4,2,8,128]{4,3,2,1,0:T(8,128)S(1)}, u32[]{:S(2)}, u32[]{:S(2)}) collective-permute-start(f32[1,4,2,8,128]{4,3,2,1,0:T(8,128)} %param.9), channel_id=1, source_target_pairs={{2,0},{0,2},{3,1},{1,3},{6,4},{4,6},{7,5},{5,7},{10,8},{8,10},{11,... | collective-permute-start | bytes 98312 | tf_op jit(solution)/shard_map/ppermute | solution.py:18
  18.3 1.3 collective-permute-start.2
  18.3 1.3 collective-permute-start.3
  20.1 2.1 copy-start.2
  25.4 71.2 %all-reduce.5.cloned.1.call-start = ((), (), s32[]{:S(2)}) async-start(), calls=%async_computation.1 | async-start | bytes 393216 | tf_op jit(solution)/shard_map/psum | solution.py:109
  370.7 276.0 %copy-start.1 = (f32[192,192]{1,0:T(8,128)}, f32[192,192]{1,0:T(8,128)S(1)}, u32[]{:S(2)}) copy-start(f32[192,192]{1,0:T(8,128)S(1)} %get-tuple-element.297) | copy-start | bytes 442372
Sparse Core Ops, SparseCore 0:
  25.5 33.6 all-reduce.2
  61.6 34.9 all-reduce.4

commit v2 on v0

--- a/solution.py
+++ b/solution.py
@@ -106,7 +106,7 @@
         lax.axis_size("snap") * lax.axis_size("slab") * lax.axis_size("sub") * bases.shape[1]
     )
     identity = jnp.eye(feature_count, dtype=jnp.float32)
-    total_gram = lax.psum(local_gram, ("snap", "slab", "sub"))
+    total_gram = jnp.sum(lax.all_gather(local_gram, ("snap", "slab", "sub")), axis=0)
     r_factor = upper_cholesky(total_gram / cells_total + ridge_value * identity)
     inverse = transposed_solve(r_factor, identity)
     solved = dot_highest(inverse, features)

time: 696 us -> 652 us (0.937)
  waiting for transfers between devices: 92.6 us -> 47.4 us
    psum x1 -> x0, waiting for transfers between devices: 92.5 us -> none  [local(): total_gram = lax.psum(local_gram, ('snap', 'slab', 'sub'))]
    all_gather x0 -> x1, waiting for transfers between devices: none -> 47.3 us  [local(): lax.all_gather(local_gram, ('snap', 'slab', 'sub'))]
where the time goes in v2:
time: 652 us; the launch traced here: 648 us
  local copies, waits for them, and re-layouts  254 us (39%)
  loops' own time  151 us (23%)
  matrix products  146 us (22%)
  waiting for transfers between devices  47.4 us (7%)
  other arithmetic  30.5 us (5%)
  between operations  14.9 us (2%)
    dot_general x194, matrix products, dot_highest(): return jnp.dot(left_matrix, right_matrix, precision=lax.Precision.HIGHEST)  144 us
    another operation x1, loops' own time, upper_cholesky(): return lax.fori_loop(0, order, column_step, start)[1]  143 us
    dynamic_slice x192, local copies, waits for them, and re-layouts, row_step(): pivot = lax.dynamic_slice_in_dim(column, step, 1, 0)[0]  114 us
    dynamic_slice x192, local copies, waits for them, and re-layouts, column_step(): pivot = lax.dynamic_slice_in_dim(row_now, step, 1, 0)[0]  113 us
    all_gather x1, waiting for transfers between devices, local(): lax.all_gather(local_gram, ('snap', 'slab', 'sub'))  47.3 us
    sub x192, other arithmetic, column_step(): work = work - scaled[:, None] * scaled[None, :]  19.5 us
  transfers between devices with their start and end apart: 5, of which 2 were waited for; matrix products, arithmetic and copies ran while one was open for 1% of the time, Pallas kernels for 0%

profile of v2, /device:TPU:0, one launch (start us, length us, event | category | flops | bytes accessed | tf_op | source)
XLA Modules:
  0.0 647.7 jit_solution(13571493129565778613)
XLA Ops:
  7.2 3.0 collective-permute-start.1
  10.3 0.8 bitcast_dynamic-update-slice_fusion.2
  11.1 0.9 slice_bitcast_fusion.7
  12.0 0.9 slice_bitcast_fusion.6
  12.9 0.9 slice_bitcast_fusion.3
  13.9 0.9 slice_bitcast_fusion.2
  15.4 1.3 fusion.15
  16.7 0.8 eq.29
  17.5 0.8 constant_dynamic-update-slice_fusion.1
  18.8 0.7 bitcast_dynamic-update-slice_fusion.1
  20.1 2.1 fusion.8
  22.2 1.1 fusion.6
  23.3 2.1 fusion.17
  25.4 47.3 %all-gather.3.cloned.1.call-done = f32[3072,192]{1,0:T(8,128)} async-done(((f32[192,192]{1,0:T(8,128)}), f32[3072,192]{1,0:T(8,128)}) %all-gather.3.cloned.1.call-update) | async-done | bytes 2359312 | tf_op jit(solution)/shard_map/all_gather | solution.py:109
  72.7 2.1 reduce_sum.19
  74.9 288.9 %while.36 = (s32[]{:T(128)}, f32[192,192]{1,0:T(8,128)S(1)}, f32[192,192]{1,0:T(8,128)S(1)}, s32[]{:T(128)}, s32[]{:T(128)}, /*index=5*/s32[]{:T(128)}) while((s32[]{:T(128)}, f32[192,192]{1,0:T(8,128)S(1)}, f32[192,192]{1,0:T(8,128)S(1)}, s32[]{:T(128)}, s32[]{:T(128)}, /*index=5*/s32[]{:T(128)}) %tuple.96), condition=%wide.region_3.4_spmd.clone, body=%wide.region_2.3_spmd.clone.sunk | while | flops 74691 | bytes 302333 | solution.py:49
  364.0 274.4 %while.37 = (s32[]{:T(128)}, f32[192,192]{1,0:T(8,128)S(1)}, f32[192,192]{1,0:T(8,128)S(1)}, f32[192,192]{0,1:T(8,128)S(1)}, s32[]{:T(128)}, /*index=5*/s32[]{:T(128)}, s32[]{:T(128)}) while((s32[]{:T(128)}, f32[192,192]{1,0:T(8,128)S(1)}, f32[192,192]{1,0:T(8,128)S(1)}, f32[192,192]{0,1:T(8,128)S(1)}, s32[]{:T(128)}, ...), condition=%wide.region_5.6_spmd.clone, body=%wide.region_4.5_spmd.clone.sunk | while | flops 443139 | bytes 154493 | solution.py:64
  366.0 0.7 fusion.30
  368.9 0.7 fusion.30
  373.2 0.7 fusion.30
  377.5 0.7 fusion.30
  384.6 0.7 fusion.30
  638.3 1.5 fusion.7
  639.8 1.1 copy.23
  (2137 shorter events, 409.5 us)
Async XLA Ops:
  7.2 12.7 %copy-start = (f32[1,4,2,8,128]{4,3,2,1,0:T(8,128)S(1)}, f32[1,4,2,8,128]{4,3,2,1,0:T(8,128)}, u32[]{:S(2)}) copy-start(f32[1,4,2,8,128]{4,3,2,1,0:T(8,128)} %param.9) | copy-start | bytes 98308
  7.2 65.5 %all-gather.3.cloned.1.call-start = ((), (), s32[]{:S(2)}) async-start(), calls=%async_computation | async-start | bytes 3342336 | tf_op jit(solution)/shard_map/all_gather | solution.py:109
  7.2 10.2 %collective-permute-start.1 = (f32[1,4,2,8,128]{4,3,2,1,0:T(8,128)}, f32[1,4,2,8,128]{4,3,2,1,0:T(8,128)S(1)}, u32[]{:S(2)}, u32[]{:S(2)}) collective-permute-start(f32[1,4,2,8,128]{4,3,2,1,0:T(8,128)} %param.9), channel_id=1, source_target_pairs={{0,2},{2,0},{1,3},{3,1},{4,6},{6,4},{5,7},{7,5},{8,10},{10,8},{9,1... | collective-permute-start | bytes 98312 | tf_op jit(solution)/shard_map/ppermute | solution.py:15
  10.3 8.0 %collective-permute-start = (f32[1,4,2,8,128]{4,3,2,1,0:T(8,128)}, f32[1,4,2,8,128]{4,3,2,1,0:T(8,128)S(1)}, u32[]{:S(2)}, u32[]{:S(2)}) collective-permute-start(f32[1,4,2,8,128]{4,3,2,1,0:T(8,128)} %param.9), channel_id=1, source_target_pairs={{2,0},{0,2},{3,1},{1,3},{6,4},{4,6},{7,5},{5,7},{10,8},{8,10},{11,... | collective-permute-start | bytes 98312 | tf_op jit(solution)/shard_map/ppermute | solution.py:18
  18.3 1.3 collective-permute-start.2
  18.3 1.3 collective-permute-start.3
  20.1 2.1 copy-start.2
  363.8 276.0 %copy-start.1 = (f32[192,192]{1,0:T(8,128)}, f32[192,192]{1,0:T(8,128)S(1)}, u32[]{:S(2)}) copy-start(f32[192,192]{1,0:T(8,128)S(1)} %get-tuple-element.297) | copy-start | bytes 442372
Sparse Core Ops, SparseCore 0:
  25.5 47.1 all-gather.2
